TPU v7x, 32 devices: a whole 2x2x4 slice. The times are simulated.
32 devices in a mesh: dp: 8 (over z, x), mp: 4 (over y, core).
Axes of the slice: x: 2, y: 2, z: 4, core: 2. Of those that a mesh axis runs over, the one named last changes fastest.
Arguments:
- patches: bfloat16 [12704, 768], P('dp'), may hold values from -6 to 6
- norm1_gain: float32 [768], replicated, may hold values from 0.5 to 1.5
- norm1_bias: float32 [768], replicated, may hold values from -1.75 to 1.75
- qkv_weight: bfloat16 [768, 3, 768], P(None, None, 'mp'), may hold values from -0.21875 to 0.21875
- qv_bias: float32 [2, 768], P(None, 'mp'), may hold values from -1.25 to 1.25
- out_weight: bfloat16 [768, 768], P('mp'), may hold values from -0.875 to 0.875
- out_bias: float32 [768], replicated, may hold values from -1.75 to 1.75
- norm2_gain: float32 [768], replicated, may hold values from 0.5 to 1.5
- norm2_bias: float32 [768], replicated, may hold values from -1.75 to 1.75
- up_weight: bfloat16 [768, 3072], P(None, 'mp'), may hold values from -0.21875 to 0.21875
- up_bias: float32 [3072], P('mp'), may hold values from -3 to 3
- down_weight: bfloat16 [3072, 768], P('mp'), may hold values from -0.109375 to 0.109375
- down_bias: float32 [768], replicated, may hold values from -1.75 to 1.75
- dec_weight: bfloat16 [768, 512], P(None, 'mp'), may hold values from -0.21875 to 0.21875
- dec_bias: float32 [512], P('mp'), may hold values from -3 to 3
- mask_token: float32 [512], P('mp'), may hold values from -6 to 6
- lengths: int32 [32], replicated, may hold values from 40 to 529, as said below
- blank: int32 [32, 529], replicated, may hold values from 0 to 1, as said below
- visible: int32 [32, 397], replicated, may hold values from 0 to 528, as said below
- plan: int32 [32], replicated, may hold values from 0 to 7, as said below
- dec_cot: bfloat16 [32, 529, 512], P('dp', None, 'mp'), may hold values from -6 to 6
Outputs:
- decoder_input: bfloat16 [32, 529, 512], P('dp', None, 'mp')
- patches_grad: float32 [12704, 768], P('dp')
- norm1_gain_grad: float32 [768], replicated
- norm1_bias_grad: float32 [768], replicated
- qkv_weight_grad: float32 [768, 3, 768], P(None, None, 'mp')
- qv_bias_grad: float32 [2, 768], P(None, 'mp')
- out_weight_grad: float32 [768, 768], P('mp')
- out_bias_grad: float32 [768], replicated
- norm2_gain_grad: float32 [768], replicated
- norm2_bias_grad: float32 [768], replicated
- up_weight_grad: float32 [768, 3072], P(None, 'mp')
- up_bias_grad: float32 [3072], P('mp')
- down_weight_grad: float32 [3072, 768], P('mp')
- down_bias_grad: float32 [768], replicated
- dec_weight_grad: float32 [768, 512], P(None, 'mp')
- dec_bias_grad: float32 [512], P('mp')
- mask_token_grad: float32 [512], P('mp')
Inputs may be any that keep to these rules, and one draw needn't show every extreme that they name: `lengths`: one strip in every draw has 529 text patches and another 40. blank[j, 0] is 0. `visible`: each row holds 397 distinct positions in increasing order, the first of them 0. `plan`: each data index is named by exactly 4 strips, and never by two strips of the same owner.
All inputs are finite; a program needn't handle non-finite values.
Results may differ from a plain program's by a relative error of at most 0.02.
Values may be sent and summed in bfloat16 or wider, within the bound.
A program may use at most 128 MiB of HBM per device.

v0:
```python
from functools import partial

import jax
import jax.numpy as jnp
import numpy as np
from jax import lax
from jax.experimental import pallas as pl
from jax.experimental.pallas import tpu as pltpu
from jax.sharding import PartitionSpec as P

HD = 64
EPSILON = 1e-06
NEGATIVE = -1e30
F32 = jnp.float32
BF16 = jnp.bfloat16


def nn(a, b):
    return lax.dot_general(a, b, (((1,), (0,)), ((), ())), preferred_element_type=F32)


def tn(a, b):
    return lax.dot_general(a, b, (((0,), (0,)), ((), ())), preferred_element_type=F32)


def nt(a, b):
    return lax.dot_general(a, b, (((1,), (1,)), ((), ())), preferred_element_type=F32)


def norm_stats(inputs):
    centered = inputs - jnp.mean(inputs, -1, keepdims=True)
    inverse = lax.rsqrt(jnp.mean(centered * centered, -1, keepdims=True) + EPSILON)
    return centered * inverse, inverse


def norm_backward(incoming, normed, inverse, gain_vec):
    weighted = incoming * gain_vec
    inner = (
        weighted
        - jnp.mean(weighted, -1, keepdims=True)
        - normed * jnp.mean(weighted * normed, -1, keepdims=True)
    )
    return inner * inverse, jnp.sum(incoming * normed, 0), jnp.sum(incoming, 0)


def prepare_kernel(count, held_ref, len_ref, *refs):
    pos_ref, cot_ref, vis_ref, blank_ref, patches_ref, out_ref, mask_ref, bias_ref, x_ref = refs

    @pl.when(pl.program_id(0) == 0)
    def _():
        mask_ref[...] = jnp.zeros_like(mask_ref)

    seq = cot_ref.shape[1]
    n, _, chunk, feats = out_ref.shape
    rows = bias_ref.shape[2]
    spot = lax.broadcasted_iota(jnp.int32, (n * chunk, seq), 1)
    chosen = (pos_ref[0] == spot).astype(F32)
    picked = nn(chosen.astype(BF16), cot_ref[0])
    out_ref[...] = picked.astype(BF16).reshape(n, 1, chunk, feats)
    hidden = 1.0 - jnp.sum(chosen, 0, keepdims=True)
    hidden = jnp.broadcast_to(hidden, (8, seq)).astype(BF16)
    mask_ref[...] += nn(hidden, cot_ref[0])
    place = lax.broadcasted_iota(jnp.int32, (1, seq), 1)
    usable = (blank_ref[0] == 0) & (place < len_ref[pl.program_id(0)])
    usable = jnp.broadcast_to(usable.astype(F32), (8, seq)).astype(BF16)
    at = lax.broadcasted_iota(jnp.int32, (seq, rows), 0)
    allowed = nn(usable, (vis_ref[0] == at).astype(F32).astype(BF16))
    bias_ref[0] = jnp.where(allowed[:1] > 0.5, 0.0, NEGATIVE)
    for s in range(patches_ref.shape[0] // count):

        @pl.when(pl.program_id(0) == s)
        def _():
            first, last = s * count, (s + 1) * count
            start = first // 16 * 16
            block = patches_ref[start:last].astype(F32)[first - start :]
            filler = jnp.zeros((rows - count, block.shape[1]), F32)
            x_ref[0] = jnp.concatenate([block, filler]).astype(BF16)


def prepare(held_strips, lengths, pos_col, cot, vis, blank, patches, n, chunk):
    held, seq, feats = cot.shape
    rows = vis.shape[2]
    width = patches.shape[1]
    return pl.pallas_call(
        partial(prepare_kernel, patches.shape[0] // held),
        grid_spec=pltpu.PrefetchScalarGridSpec(
            num_scalar_prefetch=2,
            grid=(held,),
            in_specs=[
                pl.BlockSpec((1, n * chunk, 1), lambda s, h, l: (s, 0, 0)),
                pl.BlockSpec((1, seq, feats), lambda s, h, l: (s, 0, 0)),
                pl.BlockSpec((1, 1, rows), lambda s, h, l: (h[s], 0, 0)),
                pl.BlockSpec((1, 1, seq), lambda s, h, l: (h[s], 0, 0)),
                pl.BlockSpec(patches.shape, lambda s, h, l: (0, 0)),
            ],
            out_specs=[
                pl.BlockSpec((n, 1, chunk, feats), lambda s, h, l: (0, s, 0, 0)),
                pl.BlockSpec((8, feats), lambda s, h, l: (0, 0)),
                pl.BlockSpec((1, 1, rows), lambda s, h, l: (s, 0, 0)),
                pl.BlockSpec((1, rows, width), lambda s, h, l: (s, 0, 0)),
            ],
        ),
        out_shape=[
            jax.ShapeDtypeStruct((n, held, chunk, feats), BF16),
            jax.ShapeDtypeStruct((8, feats), F32),
            jax.ShapeDtypeStruct((held, 1, rows), F32),
            jax.ShapeDtypeStruct((held, rows, width), BF16),
        ],
        name="prepare",
        compiler_params=pltpu.CompilerParams(vmem_limit_bytes=24 << 20),
    )(held_strips, lengths, pos_col, cot, vis, blank, patches)


def finish_kernel(vis, pos_ref, rows_ref, token_ref, patch_ref, up_ref, down_ref, *outs):
    out_ref, patches_ref, up_out, down_out = outs
    n, _, chunk, feats = rows_ref.shape
    seq = out_ref.shape[1]
    spot = lax.broadcasted_iota(jnp.int32, (seq, n * chunk), 0)
    chosen = (pos_ref[0] == spot).astype(F32)
    rows = nn(chosen.astype(BF16), rows_ref[...].reshape(n * chunk, feats))
    hidden = 1.0 - jnp.sum(chosen, 1, keepdims=True)
    token = token_ref[...].reshape(1, feats).astype(BF16).astype(F32)
    out_ref[0] = (rows + hidden * token).astype(BF16)
    up_out[...] = up_ref[...].astype(F32)
    down_out[...] = down_ref[...].astype(F32)
    for s in range(patches_ref.shape[0] // vis):

        @pl.when(pl.program_id(0) == s)
        def _():
            patches_ref[s * vis : (s + 1) * vis] = patch_ref[0, :vis].astype(F32)


def finish(pos_row, rows, token, patch_all, up_grad, down_grad, seq, vis):
    n, held, chunk, feats = rows.shape
    _, each, width = patch_all.shape
    tall = width // held
    whole = pl.BlockSpec((held * vis, width), lambda s: (0, 0))
    tile = pl.BlockSpec((tall, width), lambda s: (s, 0))
    shape = jax.ShapeDtypeStruct
    return pl.pallas_call(
        partial(finish_kernel, vis),
        grid=(held,),
        in_specs=[
            pl.BlockSpec((1, 1, n * chunk), lambda s: (s, 0, 0)),
            pl.BlockSpec((n, 1, chunk, feats), lambda s: (0, s, 0, 0)),
            pl.BlockSpec(memory_space=pltpu.VMEM),
            pl.BlockSpec((1, each, width), lambda s: (s, 0, 0)),
            tile,
            tile,
        ],
        out_specs=[pl.BlockSpec((1, seq, feats), lambda s: (s, 0, 0)), whole, tile, tile],
        out_shape=[
            shape((held, seq, feats), BF16),
            shape((held * vis, width), F32),
            shape((width, width), F32),
            shape((width, width), F32),
        ],
        name="finish",
        compiler_params=pltpu.CompilerParams(vmem_limit_bytes=32 << 20),
    )(pos_row, rows, token, patch_all, up_grad, down_grad)


MESH = pl.DeviceIdType.MESH


class Wires:
    def __init__(self, send, recv):
        self.send, self.recv, self.used = send, recv, 0

    def take(self, count=1):
        first = self.used
        self.used += count
        return first

    def copy(self, src, dst, target, index=None):
        index = self.take() if index is None else index
        return pltpu.make_async_remote_copy(
            src_ref=src,
            dst_ref=dst,
            send_sem=self.send.at[index],
            recv_sem=self.recv.at[index],
            device_id=target,
            device_id_type=MESH,
        )


class Place:
    def __init__(self, n):
        self.n = n
        self.d = lax.axis_index("dp")
        self.m = lax.axis_index("mp")
        self.core, self.y = self.m % 2, self.m // 2
        self.core_peer = (self.d, self.m + 1 - 2 * self.core)
        self.y_peer = (self.d, (self.m + 2) % 4)
        self.far_peer = (self.d, 3 - self.m)
        self.y_strip = (self.m + 2) % 4

    def strip(self, i):
        y = self.y + (1 - 2 * self.y) * (1 - i // 2)
        core = self.core + (1 - 2 * self.core) * (1 - i % 2)
        return 2 * y + core

    def dp_peer(self, k):
        return ((self.d + k) % self.n, self.m)


def meet_all(place):
    barrier = pltpu.get_barrier_semaphore()
    for peer in (place.core_peer, place.y_peer, place.far_peer):
        pl.semaphore_signal(barrier, inc=1, device_id=peer, device_id_type=MESH)

    def greet(k, carry):
        pl.semaphore_signal(barrier, inc=1, device_id=place.dp_peer(k), device_id_type=MESH)
        return carry

    lax.fori_loop(1, place.n, greet, 0)
    pl.semaphore_wait(barrier, place.n + 2)


class Spread:
    def __init__(self, wires, place, src, dst, blocks=True, local=True, tall=None):
        self.wires, self.place, self.src, self.blocks, self.local = wires, place, src, blocks, local
        d = place.d
        self.slot = dst.at[d] if tall is None else dst.at[pl.ds(pl.multiple_of(d * tall, tall), tall)]
        self.base = wires.take(place.n)

    def made(self, k):
        peer = self.place.dp_peer(k)
        src = self.src.at[peer[0]] if self.blocks else self.src
        return self.wires.copy(src, self.slot, peer, self.base + k)

    def start(self):
        def one(k, carry):
            self.made(k).start()
            return carry

        lax.fori_loop(1, self.place.n, one, 0)
        if self.local:
            self.slot[...] = self.src[self.place.d] if self.blocks else self.src[...]

    def wait(self):
        def one(k, carry):
            self.made(k).wait()
            return carry

        lax.fori_loop(1, self.place.n, one, 0)


class Scatter:
    def __init__(self, wires, place, core_send, core_recv, y_send, y_recv):
        self.core_send, self.core_recv, self.y_send, self.y_recv = core_send, core_recv, y_send, y_recv
        self.core = [
            wires.copy(core_send.at[i], core_recv.at[i], place.core_peer) for i in range(2)
        ]
        self.away = wires.copy(y_send, y_recv, place.y_peer)

    def give_core(self, i, value):
        self.core_send[i] = value.astype(BF16)
        self.core[i].start()

    def give_y(self, value):
        self.core[0].wait_recv()
        self.y_send[...] = (value + self.core_recv[0].astype(F32)).astype(BF16)

    def own(self, value, arrived=False):
        self.core[1].wait_recv()
        if not arrived:
            self.away.wait_recv()
        return value + self.core_recv[1].astype(F32) + self.y_recv[...].astype(F32)

    def close(self):
        for made in (*self.core, self.away):
            made.wait_send()


class Gather:
    def __init__(self, wires, place, full, src=None):
        spot, passing = full.at[place.m], full.at[place.y_strip]
        src = spot if src is None else src
        self.over_y = wires.copy(src, spot, place.y_peer)
        self.over_core = wires.copy(src, spot, place.core_peer)
        self.passed = wires.copy(passing, passing, place.core_peer)

    def start(self):
        self.over_y.start()
        self.over_core.start()

    def forward(self):
        self.over_y.wait_recv()
        self.passed.start()

    def wait(self):
        self.over_core.wait_recv()
        self.passed.wait_recv()

    def close(self):
        for made in (self.over_y, self.over_core, self.passed):
            made.wait_send()


class Reduce:
    def __init__(self, wires, place, g, recv, h, bits):
        self.g, self.recv, self.h = g, recv, h
        n = place.n
        base, size = 0, n
        self.halves, self.doubles, path = [], [], []
        for k in bits:
            half = size // 2
            bit = (place.d // (1 << k)) % 2
            peer = (place.d + (1 - 2 * bit) * (1 << k), place.m)
            keep, away, landing = base + bit * half, base + (1 - bit) * half, n - size
            made = wires.copy(g.at[pl.ds(away, half)], recv.at[pl.ds(landing, half)], peer)
            self.halves.append((made, keep, landing, half))
            path.append((base, peer))
            base, size = keep, half
        self.mine = base
        for start, peer in reversed(path):
            held = h.at[pl.ds(base, size)]
            self.doubles.append(wires.copy(held, held, peer))
            base, size = start, size * 2

    def steps(self):
        g, recv, h = self.g, self.recv, self.h
        for made, keep, landing, half in self.halves:
            made.start()
            yield
            made.wait_recv()

            def add(i, carry):
                total = g[keep + i].astype(F32) + recv[landing + i].astype(F32)
                g[keep + i] = total.astype(BF16)
                return carry

            lax.fori_loop(0, half, add, 0)
        h[self.mine] = g[self.mine]
        for made in self.doubles:
            made.start()
            yield
            made.wait_recv()
        for made in [half[0] for half in self.halves] + self.doubles:
            made.wait_send()


class Group:
    def __init__(self, sums):
        self.todo = [one.steps() for one in sums]

    def go(self):
        self.todo = [steps for steps in self.todo if next(steps, self) is not self]
        return bool(self.todo)


def layer_kernel(
    n,
    order_in,
    order_out,
    x_ref,
    gain1_ref,
    shift1_ref,
    qkv_w_ref,
    qv_b_ref,
    out_w_ref,
    out_b_ref,
    gain2_ref,
    shift2_ref,
    up_w_ref,
    up_b_ref,
    down_w_ref,
    down_b_ref,
    dec_w_ref,
    dec_b_ref,
    bias_ref,
    cot_ref,
    spot_row,
    spot_col,
    mask_ref,
    patch_hbm,
    h_up,
    h_down,
    h_at,
    h_dec,
    hop4,
    vec_ref,
    qkv,
    att,
    stat,
    mid,
    low2,
    act,
    slope,
    g3_low,
    mid_all,
    g_full,
    decs,
    a_cs,
    a_cr,
    a_ys,
    a_yr,
    b_cs,
    b_cr,
    b_ys,
    b_yr,
    own_a,
    own_b,
    own_c,
    acc,
    g_up,
    g_down,
    g_at,
    g_dec,
    r_up,
    r_down,
    r_at,
    r_dec,
    hop1,
    send2,
    hop2,
    v_own,
    w_own,
    w_all,
    copy_sem,
    send_sem,
    recv_sem,
):
    place = Place(n)
    wires = Wires(send_sem, recv_sem)
    held, rows, width = x_ref.shape
    lw = att.shape[2]
    chunk, feats = hop4.shape[2:]
    scale = HD ** (-0.5)
    row = lambda ref: ref[...].reshape(1, -1)
    total = lambda v: jnp.sum(v, 0, keepdims=True)
    m = place.m
    temp = acc.at[pl.ds(0, rows)]
    fin_all, patch_all, send3, hop3 = g3_low, act, send2, hop1

    decs_in = Gather(wires, place, decs, dec_w_ref)
    cot_one = Spread(wires, place, cot_ref, hop1)
    cot_two = Spread(wires, place, send2, hop2)
    att_sum = Scatter(wires, place, a_cs, a_cr, a_ys, a_yr)
    low2_in = Gather(wires, place, low2)
    g_in = Gather(wires, place, g_full)
    ff_sum = Scatter(wires, place, b_cs, b_cr, b_ys, b_yr)
    h2_sum = Scatter(wires, place, a_cs, a_cr, a_ys, a_yr)
    mid_in = Gather(wires, place, mid_all)
    fin_in = Gather(wires, place, fin_all)
    h1_sum = Scatter(wires, place, a_cs, a_cr, a_ys, a_yr)
    patch_in = Gather(wires, place, patch_all)
    out_one = Spread(wires, place, send3, hop3)
    out_two = Spread(wires, place, send3, hop4)
    told = Spread(wires, place, v_own, acc, blocks=False, tall=v_own.shape[0])
    shared = [
        wires.copy(w_own, w_all.at[m], peer)
        for peer in (place.core_peer, place.y_peer, place.far_peer)
    ]
    bits = list(range(n.bit_length() - 1))
    turned = [bits[1], bits[0], *bits[2:]]
    pieces = g_up.shape[0]
    ways = [bits, turned] if pieces > 1 else [bits]


    def group(g, recv, h):
        return Group(
            [Reduce(wires, place, g.at[i], recv.at[i], h.at[i], ways[i]) for i in range(pieces)]
        )

    up, down, at = group(g_up, r_up, h_up), group(g_down, r_down, h_down), group(g_at, r_at, h_at)
    dec = Group([Reduce(wires, place, g_dec, r_dec, h_dec, bits)])

    meet_all(place)
    decs_in.start()
    decs[m] = dec_w_ref[...]
    cot_one.start()

    def regroup(order_ref, src, dst):
        def one(k, carry):
            j = order_ref[k]
            dst[k // held, k % held] = src[j // held, j % held]
            return carry

        lax.fori_loop(0, n * held, one, 0)

    qkv_shift = jnp.concatenate([qv_b_ref[0:1], jnp.zeros((1, lw), F32), qv_b_ref[1:2]], 1)
    lane = lax.broadcasted_iota(jnp.int32, (1, 3 * lw), 1)
    qkv_scale = jnp.where(lane < lw, scale, 1.0)

    def low_one(s):
        normed, _ = norm_stats(x_ref[s].astype(F32))
        return (normed * row(gain1_ref) + row(shift1_ref)).astype(BF16)

    def attention(i, carry):
        s = place.strip(i)
        proj = (nn(low_one(s), qkv_w_ref[...]) + qkv_shift) * qkv_scale
        qkv[s] = proj.astype(BF16)
        bias = bias_ref[s]
        outs = []
        spot = lax.broadcasted_iota(jnp.int32, (rows, 128), 1)
        stats = jnp.zeros((rows, 128), F32)
        for h in range(lw // HD):
            q = qkv[s, :, h * HD : (h + 1) * HD]
            k = qkv[s, :, lw + h * HD : lw + (h + 1) * HD]
            v = qkv[s, :, 2 * lw + h * HD : 2 * lw + (h + 1) * HD]
            scores = nt(q, k) + bias
            top = jnp.max(scores, -1, keepdims=True)
            e = jnp.exp(scores - top)
            norm = jnp.sum(e, -1, keepdims=True)
            outs.append((nn(e.astype(BF16), v) / norm).astype(BF16))
            stats = jnp.where(spot == h, top + jnp.log(norm), stats)
        att[s] = jnp.concatenate(outs, -1)
        stat[s] = stats
        temp[...] = nn(att[s], out_w_ref[...])

        @pl.when(i == 0)
        def _():
            att_sum.give_core(0, temp[...])

        @pl.when(i == 1)
        def _():
            att_sum.give_y(temp[...])
            decs_in.forward()
            att_sum.away.start()

        @pl.when(i == 2)
        def _():
            att_sum.give_core(1, temp[...])
            cot_one.wait()
            regroup(order_in, hop1, send2)
            cot_two.start()

        return carry

    lax.fori_loop(0, held, attention, 0)
    mid[...] = x_ref[m].astype(F32) + row(out_b_ref) + att_sum.own(temp[...])
    normed, _ = norm_stats(mid[...])
    low2[m] = (normed * row(gain2_ref) + row(shift2_ref)).astype(BF16)
    low2_in.start()
    att_sum.close()
    cot_two.wait()
    t = lax.broadcasted_iota(jnp.int32, (rows, n * chunk), 0)
    sel = (t == spot_row[...]).astype(F32).astype(BF16)
    for s in range(held):
        g_full[m, s] = nn(sel, hop2[:, s].reshape(n * chunk, feats)).astype(BF16)
    decs_in.wait()
    v_own[...] = jnp.zeros_like(v_own)
    low2_in.forward()
    g_in.start()
    low2_in.wait()

    tall = 16

    def feed_forward(i, carry):
        s = place.strip(i)
        temp[...] = nn(low2[s], up_w_ref[...]) + row(up_b_ref)

        def some(r, inner):
            at = pl.ds(pl.multiple_of(r * tall, tall), tall)
            pre = temp[at]
            half = 0.5 * (1.0 + lax.erf(pre * np.float32(0.5**0.5)))
            bell = jnp.exp(-0.5 * pre * pre) * np.float32((2 * np.pi) ** -0.5)
            act[s, at] = (pre * half).astype(BF16)
            slope[s, at] = (half + pre * bell).astype(BF16)
            return inner

        lax.fori_loop(0, rows // tall, some, 0)
        temp[...] = nn(act[s], down_w_ref[...])

        @pl.when(i == 0)
        def _():
            ff_sum.give_core(0, temp[...])

        @pl.when(i == 1)
        def _():
            ff_sum.give_y(temp[...])
            g_in.forward()
            ff_sum.away.start()

        @pl.when(i == 2)
        def _():
            ff_sum.give_core(1, temp[...])

        @pl.when(i == 3)
        def _():
            own_b[...] = temp[...].astype(BF16)

        return carry

    lax.fori_loop(0, held, feed_forward, 0)
    g_in.wait()

    def g_three(s):
        weight = jnp.concatenate([decs[i] for i in range(4)], 1)
        return nt(jnp.concatenate([g_full[i, s] for i in range(4)], 1), weight)

    def g_low(s, carry):
        g3_low[s] = g_three(s).astype(BF16)
        return carry

    lax.fori_loop(0, held, g_low, 0)

    def weight_grad(left, right, out):
        acc[...] = jnp.zeros_like(acc)

        def add(s, carry):
            acc[...] += tn(left[s], right[s])
            return carry

        lax.fori_loop(0, held, add, 0)
        out[...] = acc[...].reshape(out.shape).astype(BF16)

    weight_grad(act, g3_low, g_down)
    down.go()

    def backward_ff(i, carry):
        s = place.strip(i)
        g_pre = nt(g3_low[s], down_w_ref[...]) * slope[s].astype(F32)
        slope[s] = g_pre.astype(BF16)
        v_own[6:7] += total(g_pre)
        temp[...] = nt(slope[s], up_w_ref[...])

        @pl.when(i == 0)
        def _():
            h2_sum.give_core(0, temp[...])

        @pl.when(i == 1)
        def _():
            h2_sum.give_y(temp[...])
            ff_sum.away.wait_recv()
            h2_sum.away.start()
            down.go()

        @pl.when(i == 2)
        def _():
            h2_sum.give_core(1, temp[...])

        @pl.when(i == 3)
        def _():
            own_a[...] = temp[...]
            down.go()

        return carry

    lax.fori_loop(0, held, backward_ff, 0)
    weight_grad(low2, slope, g_up)
    up.go()
    final = mid[...] + ff_sum.own(own_b[...].astype(F32), arrived=True) + row(down_b_ref)
    fin_all[m] = final.astype(BF16)
    g_own = g_three(m)
    v_own[5:6] = total(g_own)

    g_h2 = h2_sum.own(own_a[...])
    normed, inverse = norm_stats(mid[...])
    g_norm, gain_sum, bias_sum = norm_backward(g_h2, normed, inverse, row(gain2_ref))
    g_mid = g_own + g_norm
    own_a[...] = g_mid
    mid_all[m] = g_mid.astype(BF16)
    mid_in.start()
    h2_sum.close()
    v_own[2:3] = gain_sum.reshape(1, width)
    v_own[3:4] = bias_sum.reshape(1, width)
    v_own[4:5] = total(g_mid)
    down.go()

    def dqkv(s):
        return slope[s, :, : 3 * lw]

    def attention_back(i, carry):
        s = place.strip(3 - i)

        @pl.when(i == 1)
        def _():
            mid_in.over_core.wait_recv()

        @pl.when(i == 2)
        def _():
            mid_in.forward()
            fin_in.start()

        @pl.when(i == 3)
        def _():
            mid_in.passed.wait_recv()

        grad = nt(mid_all[s], out_w_ref[...]).astype(BF16)
        bias = bias_ref[s]
        dq, dk, dv = [], [], []
        for h in range(lw // HD):
            q = qkv[s, :, h * HD : (h + 1) * HD]
            k = qkv[s, :, lw + h * HD : lw + (h + 1) * HD]
            v = qkv[s, :, 2 * lw + h * HD : 2 * lw + (h + 1) * HD]
            g = grad[:, h * HD : (h + 1) * HD]
            o = att[s, :, h * HD : (h + 1) * HD]
            p = jnp.exp(nt(q, k) + bias - stat[s, :, h : h + 1])
            dv.append(tn(p.astype(BF16), g).astype(BF16))
            inner = jnp.sum(g.astype(F32) * o.astype(F32), -1, keepdims=True)
            ds = (p * (nt(g, v) - inner)).astype(BF16)
            dq.append((nn(ds, k) * scale).astype(BF16))
            dk.append(tn(ds, q).astype(BF16))
        slope[s, :, : 3 * lw] = jnp.concatenate(dq + dk + dv, -1)
        temp[...] = nt(dqkv(s), qkv_w_ref[...])

        @pl.when(i == 0)
        def _():
            own_c[...] = temp[...].astype(BF16)
            up.go()

        @pl.when(i == 1)
        def _():
            h1_sum.give_core(1, temp[...])
            down.go()
            up.go()
            down.go()

        @pl.when(i == 2)
        def _():
            a_ys[...] = temp[...].astype(BF16)
            up.go()

        @pl.when(i == 3)
        def _():
            h1_sum.give_core(0, temp[...])
            h1_sum.give_y(a_ys[...].astype(F32))
            down.go()

        return carry

    lax.fori_loop(0, held, attention_back, 0)

    acc[...] = jnp.zeros_like(acc)

    def attention_grads(s, carry):
        acc[:lw] += tn(att[s], mid_all[s])
        acc[lw:] += tn(dqkv(s), low_one(s))
        return carry

    lax.fori_loop(0, held, attention_grads, 0)
    g_at[...] = acc[...].reshape(g_at.shape).astype(BF16)
    at.go()
    up.go()
    columns = jnp.zeros((1, 3 * lw), F32)
    dec_rows = jnp.zeros((1, feats), F32)
    for s in range(held):
        columns += total(dqkv(s).astype(F32))
        dec_rows += total(g_full[m, s].astype(F32))
    blank = jnp.zeros((1, width - 2 * lw - 2 * feats), F32)
    v_own[7:8] = jnp.concatenate(
        [columns[:, :lw], columns[:, 2 * lw :], dec_rows, mask_ref[0:1], blank], 1
    )

    fin_in.forward()
    h1_sum.away.start()
    fin_in.wait()
    t = lax.broadcasted_iota(jnp.int32, (n * chunk, rows), 1)
    sel = (t == spot_col[...]).astype(F32).astype(BF16)
    for s in range(held):
        projected = (nn(fin_all[s], dec_w_ref[...]) + row(dec_b_ref)).astype(BF16)
        send3[:, s] = nn(sel, projected).astype(BF16).reshape(n, chunk, feats)
    out_one.start()
    dec_grad = jnp.zeros((width, feats), F32)
    for s in range(held):
        dec_grad += tn(fin_all[s], g_full[m, s])
    g_dec[...] = dec_grad.reshape(g_dec.shape).astype(BF16)
    up.go()
    dec.go()
    at.go()
    up.go()

    g_h1 = h1_sum.own(own_c[...].astype(F32))
    normed, inverse = norm_stats(x_ref[m].astype(F32))
    g_norm, gain_sum, bias_sum = norm_backward(g_h1, normed, inverse, row(gain1_ref))
    patch_all[m] = (own_a[...] + g_norm).astype(BF16)
    patch_in.start()
    v_own[0:1] = gain_sum.reshape(1, width)
    v_own[1:2] = bias_sum.reshape(1, width)
    at.go()
    dec.go()
    out_one.wait()
    told.start()
    regroup(order_out, hop3, send3)
    out_two.start()
    at.go()
    dec.go()
    told.wait()
    w_own[...] = lax.fori_loop(
        1, n, lambda i, v: v + acc[pl.ds(pl.multiple_of(8 * i, 8), 8)], acc[0:8]
    )
    for made in shared:
        made.start()
    w_all[m] = w_own[...]
    at.go()
    dec.go()
    out_two.wait()
    for made in shared:
        made.wait()
    summed = w_all[0] + w_all[1] + w_all[2] + w_all[3]
    vec_ref[...] = jnp.concatenate([summed[:6], w_own[6:8]], 0)
    patch_in.forward()
    while any([group.go() for group in (down, up, at, dec)]):
        pass
    patch_in.wait()
    store = pltpu.make_async_copy(patch_all, patch_hbm, copy_sem)
    store.start()
    for made in (decs_in, low2_in, g_in, ff_sum, mid_in, fin_in, h1_sum, patch_in):
        made.close()
    store.wait()


def vmem(count):
    return [pl.BlockSpec(memory_space=pltpu.VMEM)] * count


def layer(n, pieces, order_in, order_out, x, *rest):
    held, rows, width = x.shape
    lw = rest[4].shape[0]
    _, _, chunk, feats = rest[-4].shape
    each = width // (pieces * n)
    shape = jax.ShapeDtypeStruct
    low = lambda *dims: pltpu.VMEM(dims, BF16)
    full = lambda *dims: pltpu.VMEM(dims, F32)
    bits = n.bit_length() - 1
    sems = 5 * n + 64 + 2 * (3 * pieces + 1) * bits
    part = (pieces, n, each, width)
    got = (pieces, n - 1, each, width)
    strips = low(held, rows, width)
    links = [low(2, rows, width), low(2, rows, width), low(rows, width), low(rows, width)]
    hop = low(n, held, chunk, feats)
    smem = pl.BlockSpec(memory_space=pltpu.SMEM)
    return pl.pallas_call(
        partial(layer_kernel, n),
        in_specs=[smem, smem] + vmem(1 + len(rest)),
        out_specs=[pl.BlockSpec(memory_space=pl.ANY)] + vmem(6),
        out_shape=[
            shape((held, rows, width), BF16),
            shape(part, BF16),
            shape(part, BF16),
            shape(part, BF16),
            shape((n, width // n, feats), BF16),
            shape((n, held, chunk, feats), BF16),
            shape((8, width), F32),
        ],
        scratch_shapes=[
            low(held, rows, 3 * lw),
            low(held, rows, lw),
            full(held, rows, 128),
            full(rows, width),
            strips,
            strips,
            strips,
            strips,
            strips,
            low(4, held, rows, feats),
            low(4, width, feats),
            *links,
            *links,
            full(rows, width),
            low(rows, width),
            low(rows, width),
            full(width, width),
            low(*part),
            low(*part),
            low(*part),
            low(n, width // n, feats),
            low(*got),
            low(*got),
            low(*got),
            low(n - 1, width // n, feats),
            hop,
            hop,
            hop,
            full(8, width),
            full(8, width),
            full(4, 8, width),
            pltpu.SemaphoreType.DMA,
            pltpu.SemaphoreType.DMA((sems,)),
            pltpu.SemaphoreType.DMA((sems,)),
        ],
        name="layer",
        compiler_params=pltpu.CompilerParams(
            collective_id=0, has_side_effects=True, vmem_limit_bytes=62 << 20
        ),
    )(order_in, order_out, x, *rest)


def shards(
    patches,
    norm1_gain,
    norm1_bias,
    qkv_weight,
    qv_bias,
    out_weight,
    out_bias,
    norm2_gain,
    norm2_bias,
    up_weight,
    up_bias,
    down_weight,
    down_bias,
    dec_weight,
    dec_bias,
    mask_token,
    lengths,
    blank,
    visible,
    plan,
    dec_cot,
):
    n = lax.axis_size("dp")
    d = lax.axis_index("dp")
    held, seq, feats = dec_cot.shape
    vis = visible.shape[1]
    strips = plan.shape[0]
    width = patches.shape[1]
    lw = qkv_weight.shape[2]
    rows = -(-vis // 16) * 16
    real = -(-vis // n)
    chunk = -(-real // 8) * 8

    strip_ids = jnp.arange(strips, dtype=jnp.int32)
    earlier = (plan[None, :] == plan[:, None]) & (strip_ids[None, :] < strip_ids[:, None])
    packed_at = plan * held + jnp.sum(earlier.astype(jnp.int32), 1)
    strip_at = jnp.sum(
        jnp.where(packed_at[None, :] == strip_ids[:, None], strip_ids[None, :], 0), 1
    )
    held_strips = lax.dynamic_slice_in_dim(strip_at, d * held, held)
    owned_pos = lax.dynamic_slice_in_dim(visible, d * held, held)
    owned_pos = jnp.pad(owned_pos, ((0, 0), (0, n * real - vis)), constant_values=-1)
    owned_pos = jnp.pad(
        owned_pos.reshape(held, n, real), ((0, 0), (0, 0), (0, chunk - real)), constant_values=-1
    )

    vis_rows = jnp.pad(visible, ((0, 0), (0, rows - vis)), constant_values=-1)
    spread_cot, mask_grad, key_bias, x_all = prepare(
        held_strips,
        lengths[held_strips],
        owned_pos.reshape(held, n * chunk, 1),
        dec_cot,
        vis_rows.reshape(strips, 1, rows),
        blank.reshape(strips, 1, seq),
        patches,
        n,
        chunk,
    )
    spot = np.arange(n * chunk)
    spot = np.where(spot % chunk < real, spot // chunk * real + spot % chunk, -1)
    pieces = 2 if width // n % 32 == 0 else 1
    patch_all, up_grad, down_grad, at_grad, dec_grad, arrived, vectors = layer(
        n,
        pieces,
        strip_at,
        packed_at,
        x_all,
        norm1_gain,
        norm1_bias,
        qkv_weight.reshape(width, 3 * lw),
        qv_bias,
        out_weight,
        out_bias,
        norm2_gain,
        norm2_bias,
        up_weight,
        up_bias,
        down_weight,
        down_bias,
        dec_weight,
        dec_bias,
        key_bias,
        spread_cot,
        jnp.asarray(spot, jnp.int32).reshape(1, n * chunk),
        jnp.asarray(spot, jnp.int32).reshape(n * chunk, 1),
        mask_grad,
    )
    decoded, patches_grad, up_grad, down_grad = finish(
        owned_pos.reshape(held, 1, n * chunk),
        arrived,
        mask_token,
        patch_all,
        up_grad.reshape(width, width),
        down_grad.reshape(width, width),
        seq,
        vis,
    )
    at_grad = at_grad.reshape(width, width)
    out_grad = at_grad[:lw].astype(F32)
    qkv_grad = at_grad[lw:].T.astype(F32).reshape(width, 3, lw)
    mixed = vectors[7]
    return (
        decoded,
        patches_grad,
        vectors[0],
        vectors[1],
        qkv_grad,
        mixed[: 2 * lw].reshape(2, lw),
        out_grad,
        vectors[4],
        vectors[2],
        vectors[3],
        up_grad,
        vectors[6],
        down_grad,
        vectors[5],
        dec_grad.reshape(width, feats).astype(F32),
        mixed[2 * lw : 2 * lw + feats],
        mixed[2 * lw + feats : 2 * lw + 2 * feats],
    )


def solution(mesh):
    return jax.shard_map(
        shards,
        mesh=mesh,
        in_specs=(
            P("dp", None),
            P(),
            P(),
            P(None, None, "mp"),
            P(None, "mp"),
            P("mp", None),
            P(),
            P(),
            P(),
            P(None, "mp"),
            P("mp"),
            P("mp", None),
            P(),
            P(None, "mp"),
            P("mp"),
            P("mp"),
            P(),
            P(),
            P(),
            P(),
            P("dp", None, "mp"),
        ),
        out_specs=(
            P("dp", None, "mp"),
            P("dp", None),
            P(),
            P(),
            P(None, None, "mp"),
            P(None, "mp"),
            P("mp", None),
            P(),
            P(),
            P(),
            P(None, "mp"),
            P("mp"),
            P("mp", None),
            P(),
            P(None, "mp"),
            P("mp"),
            P("mp"),
        ),
        check_vma=False,
    )
```

profile of v0, /device:TPU:14, one launch (start us, length us, event | category | flops | bytes accessed | tf_op | source)
XLA Modules:
  0.0 223.0 jit_solution(11405716338934155114)
XLA Ops:
  0.7 0.9 convert_reduce_fusion
  1.6 0.7 multiply_add_fusion.order_out
  2.5 0.6 gather_fusion
  3.1 0.7 constant_dynamic-slice_fusion
  4.5 1.7 copy-done.3
  6.2 3.4 %prepare.1 = (bf16[8,4,56,128]{3,2,1,0:T(8,128)(2,1)S(1)}, f32[8,128]{1,0:T(8,128)S(1)}, f32[4,1,400]{2,1,0:T(1,128)S(1)}, bf16[4,400,768]{2,1,0:T(8,128)(2,1)S(1)}) custom-call(s32[4]{0:T(128)S(1)} %get-tuple-element.106.held_ref, s32[4]{0:T(128)S(1)} %gather_fusion, s32[4,448,1]{2,1,0:T(8,128)S(1)} %reshape.113.refs_0_, ...), custom_call_target="tpu_custom_call" | custom-call | tf_op jit(solution)/shard_map/prepare/pallas_call | solution.py:84
  9.7 1.4 copy-done.1
  11.1 0.8 copy-done.6
  11.9 0.6 copy-done.8
  12.5 0.6 copy-done.9
  13.0 1.3 copy.49.qkv_w_ref
  14.4 192.1 %layer.1 = (bf16[4,400,768]{2,1,0:T(8,128)(2,1)}, bf16[2,8,48,768]{3,2,1,0:T(8,128)(2,1)}, bf16[2,8,48,768]{3,2,1,0:T(8,128)(2,1)}, bf16[2,8,48,768]{3,2,1,0:T(8...) custom-call(s32[32]{0:T(128)} %copy-done.18, s32[32]{0:T(128)} %copy-done.19, ...), custom_call_target="tpu_custom_call" | custom-call | tf_op jit(solution)/shard_map/layer/pallas_call | solution.py:826
  206.6 1.7 copy-done.2
  208.3 1.3 copy-done.4
  209.6 1.3 copy-done.5
  210.8 1.0 copy-done.7
  211.9 5.3 %finish.1 = (bf16[4,529,128]{2,1,0:T(8,128)(2,1)S(1)}, f32[1588,768]{1,0:T(8,128)}, f32[768,768]{1,0:T(8,128)}, f32[768,768]{1,0:T(8,128)}) custom-call(s32[4,1,448]{2,1,0:T(1,128)S(1)} %reshape.87.pos_ref, bf16[8,4,56,128]{3,2,1,0:T(8,128)(2,1)S(1)} %copy-done.7, f32[128]{0:T(128)S(1)} %copy-done.10, bf16[4,400,768]{2,1,0:T(8,128)(2,1)S(1)} %copy-done.2, ...), custom_call_target="tpu_custom_call" | custom-call | tf_op jit(solution)/shard_map/finish/pallas_call | solution.py:140
  217.1 1.0 copy.50
  218.1 1.3 slice_convert_fusion
  219.5 0.9 slice_convert_fusion.1
  220.3 0.8 bitcast_convert_fusion
  221.1 0.7 slice_reduce_fusion
  221.8 0.7 reshape.99
  222.4 0.5 slice_bitcast_fusion
  (44 shorter events, 1.0 us)
Async XLA Ops:
  0.7 1.8 copy-start
  0.7 3.7 %copy-start.15 = (s32[32,397]{1,0:T(8,128)S(1)}, s32[32,397]{1,0:T(8,128)}, u32[]{:S(2)}) copy-start(s32[32,397]{1,0:T(8,128)} %param.41) | copy-start | bytes 152452
  0.7 3.6 %copy-start.13 = (bf16[4,529,128]{2,0,1:T(4,128)(2,1)S(1)}, bf16[4,529,128]{2,0,1:T(4,128)(2,1)}, u32[]{:S(2)}) copy-start(bf16[4,529,128]{2,0,1:T(4,128)(2,1)} %param.43) | copy-start | bytes 1625092
  0.7 3.8 %copy-start.16 = (s32[32,529]{1,0:T(8,128)S(1)}, s32[32,529]{1,0:T(8,128)}, u32[]{:S(2)}) copy-start(s32[32,529]{1,0:T(8,128)} %param.40) | copy-start | bytes 203140
  2.3 7.3 %copy-start.19 = (s32[32]{0:T(128)}, s32[32]{0:T(128)S(1)}, u32[]{:S(2)}) copy-start(s32[32]{0:T(128)S(1)} %multiply_add_fusion.order_out) | copy-start | bytes 388
  2.4 7.2 %copy-start.18 = (s32[32]{0:T(128)}, s32[32]{0:T(128)S(1)}, u32[]{:S(2)}) copy-start(s32[32]{0:T(128)S(1)} %select_reduce_fusion.order_in) | copy-start | bytes 388
  4.5 1.7 copy-start.3
  6.2 6.8 %copy-start.12 = (bf16[768,3,192]{0,2,1:T(8,128)(2,1)S(1)}, bf16[768,3,192]{0,2,1:T(8,128)(2,1)}, u32[]{:S(2)}) copy-start(bf16[768,3,192]{0,2,1:T(8,128)(2,1)} %param.26) | copy-start | bytes 2654212
  9.6 1.4 copy-start.1
  11.1 0.8 copy-start.6
  11.9 0.6 copy-start.8
  12.5 0.6 copy-start.9
  14.4 192.2 %copy-start.10 = (f32[128]{0:T(128)S(1)}, f32[128]{0:T(128)}, u32[]{:S(2)}) copy-start(f32[128]{0:T(128)} %token_ref.1) | copy-start | bytes 1540
  206.6 1.7 copy-start.2
  208.3 1.3 copy-start.4
  209.6 1.3 copy-start.5
  210.8 1.0 copy-start.7
  211.9 6.3 %copy-start.11 = (bf16[2,8,48,768]{3,2,1,0:T(8,128)(2,1)S(1)}, bf16[2,8,48,768]{3,2,1,0:T(8,128)(2,1)}, u32[]{:S(2)}) copy-start(bf16[2,8,48,768]{3,2,1,0:T(8,128)(2,1)} %get-tuple-element.43) | copy-start | bytes 3538948
  218.1 2.2 copy-start.14
  218.1 3.0 %copy-start.17 = (f32[8,768]{1,0:T(8,128)S(1)}, f32[8,768]{1,0:T(8,128)}, u32[]{:S(2)}) copy-start(f32[8,768]{1,0:T(8,128)} %get-tuple-element.42) | copy-start | bytes 73732
where the time goes:
time: 223 us
  Pallas kernels  201 us (90%)
  local copies, waits for them, and re-layouts  16.6 us (7%)
  other arithmetic  4.75 us (2%)
    pallas_call x1, Pallas kernels, layer(): pl.pallas_call(partial(layer_kernel, n), in_specs=[smem, smem] + vmem(1 +...  192 us
    unnamed x42, local copies, waits for them, and re-layouts  11.4 us
    pallas_call x1, Pallas kernels, finish(): pl.pallas_call(partial(finish_kernel, vis), grid=(held,), in_specs=[pl.Bl...  5.26 us

commit v1 on v0

--- a/solution.py
+++ b/solution.py
@@ -111,8 +111,9 @@
     )(held_strips, lengths, pos_col, cot, vis, blank, patches)
 
 
-def finish_kernel(vis, pos_ref, rows_ref, token_ref, patch_ref, up_ref, down_ref, *outs):
-    out_ref, patches_ref, up_out, down_out = outs
+def finish_kernel(vis, pos_ref, rows_ref, token_ref, patch_ref, *refs):
+    up_ref, down_ref, at_ref, dec_ref = refs[:4]
+    out_ref, patches_ref, up_out, down_out, out_out, qkv_out, dec_out = refs[4:]
     n, _, chunk, feats = rows_ref.shape
     seq = out_ref.shape[1]
     spot = lax.broadcasted_iota(jnp.int32, (seq, n * chunk), 0)
@@ -123,6 +124,16 @@
     out_ref[0] = (rows + hidden * token).astype(BF16)
     up_out[...] = up_ref[...].astype(F32)
     down_out[...] = down_ref[...].astype(F32)
+    dec_out[...] = dec_ref[...].astype(F32)
+
+    @pl.when(pl.program_id(0) == 0)
+    def _():
+        out_out[...] = at_ref[...].astype(F32)
+
+    @pl.when(pl.program_id(0) > 0)
+    def _():
+        qkv_out[...] = at_ref[...].astype(F32)
+
     for s in range(patches_ref.shape[0] // vis):
 
         @pl.when(pl.program_id(0) == s)
@@ -130,7 +141,7 @@
             patches_ref[s * vis : (s + 1) * vis] = patch_ref[0, :vis].astype(F32)
 
 
-def finish(pos_row, rows, token, patch_all, up_grad, down_grad, seq, vis):
+def finish(pos_row, rows, token, patch_all, up_grad, down_grad, at_grad, dec_grad, seq, vis):
     n, held, chunk, feats = rows.shape
     _, each, width = patch_all.shape
     tall = width // held
@@ -147,17 +158,30 @@
             pl.BlockSpec((1, each, width), lambda s: (s, 0, 0)),
             tile,
             tile,
+            tile,
+            pl.BlockSpec((tall, feats), lambda s: (s, 0)),
         ],
-        out_specs=[pl.BlockSpec((1, seq, feats), lambda s: (s, 0, 0)), whole, tile, tile],
+        out_specs=[
+            pl.BlockSpec((1, seq, feats), lambda s: (s, 0, 0)),
+            whole,
+            tile,
+            tile,
+            pl.BlockSpec((tall, width), lambda s: (0, 0)),
+            pl.BlockSpec((tall, width), lambda s: (jnp.maximum(s - 1, 0), 0)),
+            pl.BlockSpec((tall, feats), lambda s: (s, 0)),
+        ],
         out_shape=[
             shape((held, seq, feats), BF16),
             shape((held * vis, width), F32),
             shape((width, width), F32),
             shape((width, width), F32),
+            shape((tall, width), F32),
+            shape((width - tall, width), F32),
+            shape((width, feats), F32),
         ],
         name="finish",
-        compiler_params=pltpu.CompilerParams(vmem_limit_bytes=32 << 20),
-    )(pos_row, rows, token, patch_all, up_grad, down_grad)
+        compiler_params=pltpu.CompilerParams(vmem_limit_bytes=61 << 20),
+    )(pos_row, rows, token, patch_all, up_grad, down_grad, at_grad, dec_grad)
 
 
 MESH = pl.DeviceIdType.MESH
@@ -465,7 +489,8 @@
         )
 
     up, down, at = group(g_up, r_up, h_up), group(g_down, r_down, h_down), group(g_at, r_at, h_at)
-    dec = Group([Reduce(wires, place, g_dec, r_dec, h_dec, bits)])
+    dec_one = Spread(wires, place, g_dec, r_dec)
+    dec_two = Spread(wires, place, h_dec.at[place.d], h_dec, blocks=False, local=False)
 
     meet_all(place)
     decs_in.start()
@@ -490,7 +515,7 @@
 
     def attention(i, carry):
         s = place.strip(i)
-        proj = (nn(low_one(s), qkv_w_ref[...]) + qkv_shift) * qkv_scale
+        proj = (nt(low_one(s), qkv_w_ref[...]) + qkv_shift) * qkv_scale
         qkv[s] = proj.astype(BF16)
         bias = bias_ref[s]
         outs = []
@@ -695,7 +720,7 @@
             dq.append((nn(ds, k) * scale).astype(BF16))
             dk.append(tn(ds, q).astype(BF16))
         slope[s, :, : 3 * lw] = jnp.concatenate(dq + dk + dv, -1)
-        temp[...] = nt(dqkv(s), qkv_w_ref[...])
+        temp[...] = nn(dqkv(s), qkv_w_ref[...])
 
         @pl.when(i == 0)
         def _():
@@ -759,9 +784,10 @@
         dec_grad += tn(fin_all[s], g_full[m, s])
     g_dec[...] = dec_grad.reshape(g_dec.shape).astype(BF16)
     up.go()
-    dec.go()
     at.go()
     up.go()
+    dec_one.start()
+    at.go()
 
     g_h1 = h1_sum.own(own_c[...].astype(F32))
     normed, inverse = norm_stats(x_ref[m].astype(F32))
@@ -771,13 +797,16 @@
     v_own[0:1] = gain_sum.reshape(1, width)
     v_own[1:2] = bias_sum.reshape(1, width)
     at.go()
-    dec.go()
     out_one.wait()
-    told.start()
     regroup(order_out, hop3, send3)
     out_two.start()
+    told.start()
     at.go()
-    dec.go()
+    at.go()
+    dec_one.wait()
+    dec_total = lax.fori_loop(1, n, lambda i, v: v + r_dec[i].astype(F32), r_dec[0].astype(F32))
+    h_dec[place.d] = dec_total.astype(BF16)
+    dec_two.start()
     told.wait()
     w_own[...] = lax.fori_loop(
         1, n, lambda i, v: v + acc[pl.ds(pl.multiple_of(8 * i, 8), 8)], acc[0:8]
@@ -785,16 +814,15 @@
     for made in shared:
         made.start()
     w_all[m] = w_own[...]
-    at.go()
-    dec.go()
     out_two.wait()
     for made in shared:
         made.wait()
     summed = w_all[0] + w_all[1] + w_all[2] + w_all[3]
     vec_ref[...] = jnp.concatenate([summed[:6], w_own[6:8]], 0)
     patch_in.forward()
-    while any([group.go() for group in (down, up, at, dec)]):
+    while any([group.go() for group in (down, up, at)]):
         pass
+    dec_two.wait()
     patch_in.wait()
     store = pltpu.make_async_copy(patch_all, patch_hbm, copy_sem)
     store.start()
@@ -816,7 +844,7 @@
     low = lambda *dims: pltpu.VMEM(dims, BF16)
     full = lambda *dims: pltpu.VMEM(dims, F32)
     bits = n.bit_length() - 1
-    sems = 5 * n + 64 + 2 * (3 * pieces + 1) * bits
+    sems = 7 * n + 64 + 2 * (3 * pieces + 1) * bits
     part = (pieces, n, each, width)
     got = (pieces, n - 1, each, width)
     strips = low(held, rows, width)
@@ -861,7 +889,7 @@
             low(*got),
             low(*got),
             low(*got),
-            low(n - 1, width // n, feats),
+            low(n, width // n, feats),
             hop,
             hop,
             hop,
@@ -949,7 +977,7 @@
         x_all,
         norm1_gain,
         norm1_bias,
-        qkv_weight.reshape(width, 3 * lw),
+        qkv_weight.reshape(width, 3 * lw).T,
         qv_bias,
         out_weight,
         out_bias,
@@ -967,19 +995,19 @@
         jnp.asarray(spot, jnp.int32).reshape(n * chunk, 1),
         mask_grad,
     )
-    decoded, patches_grad, up_grad, down_grad = finish(
+    decoded, patches_grad, up_grad, down_grad, out_grad, qkv_grad, dec_grad = finish(
         owned_pos.reshape(held, 1, n * chunk),
         arrived,
         mask_token,
         patch_all,
         up_grad.reshape(width, width),
         down_grad.reshape(width, width),
+        at_grad.reshape(width, width),
+        dec_grad.reshape(width, feats),
         seq,
         vis,
     )
-    at_grad = at_grad.reshape(width, width)
-    out_grad = at_grad[:lw].astype(F32)
-    qkv_grad = at_grad[lw:].T.astype(F32).reshape(width, 3, lw)
+    qkv_grad = qkv_grad.T.reshape(width, 3, lw)
     mixed = vectors[7]
     return (
         decoded,
@@ -996,7 +1024,7 @@
         vectors[6],
         down_grad,
         vectors[5],
-        dec_grad.reshape(width, feats).astype(F32),
+        dec_grad,
         mixed[2 * lw : 2 * lw + feats],
         mixed[2 * lw + feats : 2 * lw + 2 * feats],
     )

time: 223 us -> 215 us (0.964); the launches traced: 223 us -> 211 us
  Pallas kernels: 201 us -> 196 us
  local copies, waits for them, and re-layouts: 16.6 us -> 12.7 us
  other arithmetic: 4.75 us -> 1.77 us
    pallas_call x1, Pallas kernels: 192 us -> 184 us  [layer(): pl.pallas_call(partial(layer_kernel, n), in_specs=[smem, smem] + vmem(1 +...]
    pallas_call x1, Pallas kernels: 5.26 us -> 8.98 us  [finish(): pl.pallas_call(partial(finish_kernel, vis), grid=(held,), in_specs=[pl.Bl...]
    unnamed x42 -> x24, local copies, waits for them, and re-layouts: 11.4 us -> 8.29 us
where the time goes in v1:
time: 215 us; the launch traced here: 211 us
  Pallas kernels  196 us (91%)
  local copies, waits for them, and re-layouts  12.7 us (6%)
    pallas_call x1, Pallas kernels, layer(): pl.pallas_call(partial(layer_kernel, n), in_specs=[smem, smem] + vmem(1 +...  184 us
    pallas_call x1, Pallas kernels, finish(): pl.pallas_call(partial(finish_kernel, vis), grid=(held,), in_specs=[pl.Bl...  8.98 us
    unnamed x24, local copies, waits for them, and re-layouts  8.29 us

profile of v1, /device:TPU:14, one launch (start us, length us, event | category | flops | bytes accessed | tf_op | source)
XLA Modules:
  0.0 211.2 jit_solution(505472496386016582)
XLA Ops:
  0.7 0.0 copy-start
  0.7 0.9 convert_reduce_fusion
  1.6 0.7 multiply_add_fusion.order_out
  2.3 0.1 select_reduce_fusion.order_in
  2.4 0.1 compare_select_fusion
  2.5 0.6 gather_fusion
  3.1 0.7 constant_dynamic-slice_fusion
  3.9 0.1 reshape.83
  4.0 0.3 reshape.106.refs_0_
  4.3 1.1 copy.46.refs_1_
  5.5 0.1 reshape.87.refs_3_
  5.6 1.7 copy-done.2
  7.2 3.4 %prepare.1 = (bf16[8,4,56,128]{3,2,1,0:T(8,128)(2,1)S(1)}, f32[8,128]{1,0:T(8,128)S(1)}, f32[4,1,400]{2,1,0:T(1,128)S(1)}, bf16[4,400,768]{2,1,0:T(8,128)(2,1)S(1)}) custom-call(s32[4]{0:T(128)S(1)} %get-tuple-element.112.held_ref, s32[4]{0:T(128)S(1)} %gather_fusion, s32[4,448,1]{2,1,0:T(8,128)S(1)} %reshape.106.refs_0_, ...), custom_call_target="tpu_custom_call" | custom-call | tf_op jit(solution)/shard_map/prepare/pallas_call | solution.py:84
  10.7 1.4 copy-done.1
  12.1 0.8 copy-done.3
  12.9 0.6 copy-done.4
  13.5 0.6 copy-done.5
  14.1 183.5 %layer.1 = (bf16[4,400,768]{2,1,0:T(8,128)(2,1)}, bf16[2,8,48,768]{3,2,1,0:T(8,128)(2,1)}, bf16[2,8,48,768]{3,2,1,0:T(8,128)(2,1)}, bf16[2,8,48,768]{3,2,1,0:T(8...) custom-call(s32[32]{0:T(128)} %copy-done.9, s32[32]{0:T(128)} %copy-done.10, ...), custom_call_target="tpu_custom_call" | custom-call | tf_op jit(solution)/shard_map/layer/pallas_call | solution.py:854
  197.6 0.7 reshape.84.pos_ref
  198.3 9.0 %finish.1 = (bf16[4,529,128]{2,1,0:T(8,128)(2,1)}, f32[1588,768]{1,0:T(8,128)}, f32[768,768]{1,0:T(8,128)}, f32[768,768]{1,0:T(8,128)}, f32[192,768]{1,0:T(8,128...) custom-call(s32[4,1,448]{2,1,0:T(1,128)} %reshape.84.pos_ref, bf16[8,4,56,128]{3,2,1,0:T(8,128)(2,1)} %get-tuple-element.39.rows_ref, ...), custom_call_target="tpu_custom_call" | custom-call | tf_op jit(solution)/shard_map/finish/pallas_call | solution.py:151
  207.2 2.1 copy.47
  209.3 0.7 slice_reduce_fusion
  210.0 0.7 reshape.96
  210.6 0.5 slice_bitcast_fusion
  (22 shorter events, 0.1 us)
Async XLA Ops:
  0.7 1.8 copy-start
  0.7 4.7 %copy-start.6 = (s32[32,397]{1,0:T(8,128)S(1)}, s32[32,397]{1,0:T(8,128)}, u32[]{:S(2)}) copy-start(s32[32,397]{1,0:T(8,128)} %param.41) | copy-start | bytes 152452
  0.7 4.8 %copy-start.7 = (s32[32,529]{1,0:T(8,128)S(1)}, s32[32,529]{1,0:T(8,128)}, u32[]{:S(2)}) copy-start(s32[32,529]{1,0:T(8,128)} %param.40) | copy-start | bytes 203140
  2.3 8.4 %copy-start.10 = (s32[32]{0:T(128)}, s32[32]{0:T(128)S(1)}, u32[]{:S(2)}) copy-start(s32[32]{0:T(128)S(1)} %multiply_add_fusion.order_out) | copy-start | bytes 388
  2.4 8.3 %copy-start.9 = (s32[32]{0:T(128)}, s32[32]{0:T(128)S(1)}, u32[]{:S(2)}) copy-start(s32[32]{0:T(128)S(1)} %select_reduce_fusion.order_in) | copy-start | bytes 388
  5.5 1.7 copy-start.2
  10.7 1.4 copy-start.1
  12.1 0.8 copy-start.3
  12.9 0.6 copy-start.4
  13.5 0.6 copy-start.5
  198.3 11.1 %copy-start.8 = (f32[8,768]{1,0:T(8,128)S(1)}, f32[8,768]{1,0:T(8,128)}, u32[]{:S(2)}) copy-start(f32[8,768]{1,0:T(8,128)} %get-tuple-element.47) | copy-start | bytes 73732

commit v2 on v1

--- a/solution.py
+++ b/solution.py
@@ -61,10 +61,11 @@
     hidden = jnp.broadcast_to(hidden, (8, seq)).astype(BF16)
     mask_ref[...] += nn(hidden, cot_ref[0])
     place = lax.broadcasted_iota(jnp.int32, (1, seq), 1)
-    usable = (blank_ref[0] == 0) & (place < len_ref[pl.program_id(0)])
+    strip = held_ref[pl.program_id(0)]
+    usable = (blank_ref[pl.ds(strip, 1)] == 0) & (place < len_ref[strip])
     usable = jnp.broadcast_to(usable.astype(F32), (8, seq)).astype(BF16)
     at = lax.broadcasted_iota(jnp.int32, (seq, rows), 0)
-    allowed = nn(usable, (vis_ref[0] == at).astype(F32).astype(BF16))
+    allowed = nn(usable, (vis_ref[pl.ds(strip, 1)] == at).astype(F32).astype(BF16))
     bias_ref[0] = jnp.where(allowed[:1] > 0.5, 0.0, NEGATIVE)
     for s in range(patches_ref.shape[0] // count):
 
@@ -79,7 +80,7 @@
 
 def prepare(held_strips, lengths, pos_col, cot, vis, blank, patches, n, chunk):
     held, seq, feats = cot.shape
-    rows = vis.shape[2]
+    rows = vis.shape[1]
     width = patches.shape[1]
     return pl.pallas_call(
         partial(prepare_kernel, patches.shape[0] // held),
@@ -89,8 +90,8 @@
             in_specs=[
                 pl.BlockSpec((1, n * chunk, 1), lambda s, h, l: (s, 0, 0)),
                 pl.BlockSpec((1, seq, feats), lambda s, h, l: (s, 0, 0)),
-                pl.BlockSpec((1, 1, rows), lambda s, h, l: (h[s], 0, 0)),
-                pl.BlockSpec((1, 1, seq), lambda s, h, l: (h[s], 0, 0)),
+                pl.BlockSpec(vis.shape, lambda s, h, l: (0, 0)),
+                pl.BlockSpec(blank.shape, lambda s, h, l: (0, 0)),
                 pl.BlockSpec(patches.shape, lambda s, h, l: (0, 0)),
             ],
             out_specs=[
@@ -732,11 +733,11 @@
             h1_sum.give_core(1, temp[...])
             down.go()
             up.go()
+
+        @pl.when(i == 2)
+        def _():
+            a_ys[...] = temp[...].astype(BF16)
             down.go()
-
-        @pl.when(i == 2)
-        def _():
-            a_ys[...] = temp[...].astype(BF16)
             up.go()
 
         @pl.when(i == 3)
@@ -744,6 +745,7 @@
             h1_sum.give_core(0, temp[...])
             h1_sum.give_y(a_ys[...].astype(F32))
             down.go()
+            up.go()
 
         return carry
 
@@ -957,11 +959,11 @@
     vis_rows = jnp.pad(visible, ((0, 0), (0, rows - vis)), constant_values=-1)
     spread_cot, mask_grad, key_bias, x_all = prepare(
         held_strips,
-        lengths[held_strips],
+        lengths,
         owned_pos.reshape(held, n * chunk, 1),
         dec_cot,
-        vis_rows.reshape(strips, 1, rows),
-        blank.reshape(strips, 1, seq),
+        vis_rows,
+        blank,
         patches,
         n,
         chunk,

time: 215 us -> 215 us (level)
    unnamed x24 -> x22, local copies, waits for them, and re-layouts: 8.29 us -> 9.81 us
where the time goes in v2:
time: 215 us; the launch traced here: 213 us
  Pallas kernels  196 us (91%)
  local copies, waits for them, and re-layouts  14.4 us (7%)
    pallas_call x1, Pallas kernels, layer(): pl.pallas_call(partial(layer_kernel, n), in_specs=[smem, smem] + vmem(1 +...  184 us
    unnamed x22, local copies, waits for them, and re-layouts  9.81 us
    pallas_call x1, Pallas kernels, finish(): pl.pallas_call(partial(finish_kernel, vis), grid=(held,), in_specs=[pl.Bl...  8.98 us

profile of v2, /device:TPU:14, one launch (start us, length us, event | category | flops | bytes accessed | tf_op | source)
XLA Modules:
  0.0 212.9 jit_solution(10541650661298895192)
XLA Ops:
  0.7 0.9 convert_reduce_fusion
  1.6 0.7 multiply_add_fusion.order_out
  2.2 0.1 select_reduce_fusion.order_in
  2.4 0.1 dynamic_slice.7.held_ref
  2.4 0.7 constant_dynamic-slice_fusion
  3.2 0.1 reshape.77
  3.3 0.3 reshape.89.refs_0_
  3.6 1.1 copy.46.refs_1_
  4.7 0.8 pad.14.refs_2_
  5.5 1.7 copy-done.1
  7.2 0.9 copy-done.3
  8.1 0.7 copy-done.6
  8.8 3.4 %prepare.1 = (bf16[8,4,56,128]{3,2,1,0:T(8,128)(2,1)S(1)}, f32[8,128]{1,0:T(8,128)S(1)}, f32[4,1,400]{2,1,0:T(1,128)S(1)}, bf16[4,400,768]{2,1,0:T(8,128)(2,1)S(1)}) custom-call(s32[4]{0:T(128)S(1)} %dynamic_slice.7.held_ref, s32[32]{0:T(128)S(1)} %copy-done.6, s32[4,448,1]{2,1,0:T(8,128)S(1)} %reshape.89.refs_0_, bf16[4,529,128]{2,1,0:T(8,128)(2,1)S(1)} %copy.46.refs_1_, ...), custom_call_target="tpu_custom_call" | custom-call | tf_op jit(solution)/shard_map/prepare/pallas_call | solution.py:85
  12.2 1.4 copy-done
  13.6 0.8 copy-done.2
  14.4 0.6 copy-done.4
  15.0 0.6 copy-done.5
  15.6 183.8 %layer.1 = (bf16[4,400,768]{2,1,0:T(8,128)(2,1)}, bf16[2,8,48,768]{3,2,1,0:T(8,128)(2,1)}, bf16[2,8,48,768]{3,2,1,0:T(8,128)(2,1)}, bf16[2,8,48,768]{3,2,1,0:T(8...) custom-call(s32[32]{0:T(128)} %copy-done.9, s32[32]{0:T(128)} %copy-done.8, ...), custom_call_target="tpu_custom_call" | custom-call | tf_op jit(solution)/shard_map/layer/pallas_call | solution.py:856
  199.3 0.7 reshape.78.pos_ref
  200.0 9.0 %finish.1 = (bf16[4,529,128]{2,1,0:T(8,128)(2,1)}, f32[1588,768]{1,0:T(8,128)}, f32[768,768]{1,0:T(8,128)}, f32[768,768]{1,0:T(8,128)}, f32[192,768]{1,0:T(8,128...) custom-call(s32[4,1,448]{2,1,0:T(1,128)} %reshape.78.pos_ref, bf16[8,4,56,128]{3,2,1,0:T(8,128)(2,1)} %get-tuple-element.39.rows_ref, ...), custom_call_target="tpu_custom_call" | custom-call | tf_op jit(solution)/shard_map/finish/pallas_call | solution.py:152
  209.0 2.1 copy.47
  211.1 0.7 slice_reduce_fusion
  211.7 0.7 reshape.88
  212.4 0.5 slice_bitcast_fusion
  (16 shorter events, 0.1 us)
Async XLA Ops:
  2.2 9.9 %copy-start.8 = (s32[32]{0:T(128)}, s32[32]{0:T(128)S(1)}, u32[]{:S(2)}) copy-start(s32[32]{0:T(128)S(1)} %multiply_add_fusion.order_out) | copy-start | bytes 388
  2.3 9.8 %copy-start.9 = (s32[32]{0:T(128)}, s32[32]{0:T(128)S(1)}, u32[]{:S(2)}) copy-start(s32[32]{0:T(128)S(1)} %select_reduce_fusion.order_in) | copy-start | bytes 388
  5.5 1.7 copy-start.1
  7.2 0.9 copy-start.3
  8.1 0.7 copy-start.6
  12.2 1.4 copy-start
  13.6 0.8 copy-start.2
  14.4 0.6 copy-start.4
  15.0 0.6 copy-start.5
  200.0 11.1 %copy-start.7 = (f32[8,768]{1,0:T(8,128)S(1)}, f32[8,768]{1,0:T(8,128)}, u32[]{:S(2)}) copy-start(f32[8,768]{1,0:T(8,128)} %get-tuple-element.47) | copy-start | bytes 73732

commit v3 on v2

--- a/solution.py
+++ b/solution.py
@@ -785,10 +785,10 @@
     for s in range(held):
         dec_grad += tn(fin_all[s], g_full[m, s])
     g_dec[...] = dec_grad.reshape(g_dec.shape).astype(BF16)
+    dec_one.start()
     up.go()
     at.go()
     up.go()
-    dec_one.start()
     at.go()
 
     g_h1 = h1_sum.own(own_c[...].astype(F32))

time: 215 us -> 219 us (1.019)
  Pallas kernels: 196 us -> 201 us
    pallas_call x1, Pallas kernels: 184 us -> 189 us  [layer(): pl.pallas_call(partial(layer_kernel, n), in_specs=[smem, smem] + vmem(1 +...]
where the time goes in v3:
time: 219 us; the launch traced here: 218 us
  Pallas kernels  201 us (92%)
  local copies, waits for them, and re-layouts  14.4 us (7%)
    pallas_call x1, Pallas kernels, layer(): pl.pallas_call(partial(layer_kernel, n), in_specs=[smem, smem] + vmem(1 +...  189 us
    unnamed x22, local copies, waits for them, and re-layouts  9.81 us
    pallas_call x1, Pallas kernels, finish(): pl.pallas_call(partial(finish_kernel, vis), grid=(held,), in_specs=[pl.Bl...  8.98 us

profile of v3, /device:TPU:14, one launch (start us, length us, event | category | flops | bytes accessed | tf_op | source)
XLA Modules:
  0.0 218.0 jit_solution(8166930565166055870)
XLA Ops:
  0.7 0.9 convert_reduce_fusion
  1.6 0.7 multiply_add_fusion.order_out
  2.2 0.1 select_reduce_fusion.order_in
  2.4 0.1 dynamic_slice.7.held_ref
  2.4 0.7 constant_dynamic-slice_fusion
  3.2 0.1 reshape.77
  3.3 0.3 reshape.89.refs_0_
  3.6 1.1 copy.46.refs_1_
  4.7 0.8 pad.14.refs_2_
  5.5 1.7 copy-done.1
  7.2 0.9 copy-done.3
  8.1 0.7 copy-done.6
  8.8 3.4 %prepare.1 = (bf16[8,4,56,128]{3,2,1,0:T(8,128)(2,1)S(1)}, f32[8,128]{1,0:T(8,128)S(1)}, f32[4,1,400]{2,1,0:T(1,128)S(1)}, bf16[4,400,768]{2,1,0:T(8,128)(2,1)S(1)}) custom-call(s32[4]{0:T(128)S(1)} %dynamic_slice.7.held_ref, s32[32]{0:T(128)S(1)} %copy-done.6, s32[4,448,1]{2,1,0:T(8,128)S(1)} %reshape.89.refs_0_, bf16[4,529,128]{2,1,0:T(8,128)(2,1)S(1)} %copy.46.refs_1_, ...), custom_call_target="tpu_custom_call" | custom-call | tf_op jit(solution)/shard_map/prepare/pallas_call | solution.py:85
  12.2 1.4 copy-done
  13.6 0.8 copy-done.2
  14.4 0.6 copy-done.4
  15.0 0.6 copy-done.5
  15.6 188.8 %layer.1 = (bf16[4,400,768]{2,1,0:T(8,128)(2,1)}, bf16[2,8,48,768]{3,2,1,0:T(8,128)(2,1)}, bf16[2,8,48,768]{3,2,1,0:T(8,128)(2,1)}, bf16[2,8,48,768]{3,2,1,0:T(8...) custom-call(s32[32]{0:T(128)} %copy-done.9, s32[32]{0:T(128)} %copy-done.8, ...), custom_call_target="tpu_custom_call" | custom-call | tf_op jit(solution)/shard_map/layer/pallas_call | solution.py:856
  204.4 0.7 reshape.78.pos_ref
  205.1 9.0 %finish.1 = (bf16[4,529,128]{2,1,0:T(8,128)(2,1)}, f32[1588,768]{1,0:T(8,128)}, f32[768,768]{1,0:T(8,128)}, f32[768,768]{1,0:T(8,128)}, f32[192,768]{1,0:T(8,128...) custom-call(s32[4,1,448]{2,1,0:T(1,128)} %reshape.78.pos_ref, bf16[8,4,56,128]{3,2,1,0:T(8,128)(2,1)} %get-tuple-element.39.rows_ref, ...), custom_call_target="tpu_custom_call" | custom-call | tf_op jit(solution)/shard_map/finish/pallas_call | solution.py:152
  214.1 2.1 copy.47
  216.1 0.7 slice_reduce_fusion
  216.8 0.7 reshape.88
  217.5 0.5 slice_bitcast_fusion
  (16 shorter events, 0.1 us)
Async XLA Ops:
  2.2 9.9 %copy-start.8 = (s32[32]{0:T(128)}, s32[32]{0:T(128)S(1)}, u32[]{:S(2)}) copy-start(s32[32]{0:T(128)S(1)} %multiply_add_fusion.order_out) | copy-start | bytes 388
  2.3 9.8 %copy-start.9 = (s32[32]{0:T(128)}, s32[32]{0:T(128)S(1)}, u32[]{:S(2)}) copy-start(s32[32]{0:T(128)S(1)} %select_reduce_fusion.order_in) | copy-start | bytes 388
  5.5 1.7 copy-start.1
  7.2 0.9 copy-start.3
  8.1 0.7 copy-start.6
  12.2 1.4 copy-start
  13.6 0.8 copy-start.2
  14.4 0.6 copy-start.4
  15.0 0.6 copy-start.5
  205.1 11.1 %copy-start.7 = (f32[8,768]{1,0:T(8,128)S(1)}, f32[8,768]{1,0:T(8,128)}, u32[]{:S(2)}) copy-start(f32[8,768]{1,0:T(8,128)} %get-tuple-element.47) | copy-start | bytes 73732
